TPU v7x, 1024 devices: a whole 8x8x8 slice. The times are simulated.
1024 devices in a mesh: section: 64 (over x, z), head: 16 (over y, core).
Axes of the slice: x: 8, y: 8, z: 8, core: 2. Of those that a mesh axis runs over, the one named last changes fastest.
Arguments:
- entering: bfloat16 [64, 128, 4096], P('section', None, 'head'), may hold values from -6 to 6, as said below
- fresh_slice: bfloat16 [128, 4096], P(None, 'head'), may hold values from -6 to 6
- norm_gain: float32 [64, 4096], P('section'), may hold values from 0.5 to 1.5
- w_query: bfloat16 [64, 4096, 4096], P('section', None, 'head'), may hold values from -18.8125 to 18.8125
- w_key_value: bfloat16 [64, 4096, 1024], P('section', None, 'head'), may hold values from -0.0625 to 0.0625
- doc_lengths: int32 [65], replicated, may hold values from 1 to 512, 8320 in all
Outputs:
- leaving: bfloat16 [64, 128, 4096], P('section', None, 'head')
Inputs may be any that keep to these rules, and one draw needn't show every extreme that they name: `entering`: entries of the activations that enter.
All inputs are finite; a program needn't handle non-finite values.
Results may differ from a plain program's by a relative error of at most 0.01.
Values may be sent and summed in bfloat16 or wider, within the bound.
A program may use at most 32 MiB of HBM per device.

v0:
```python
import math

import jax
import jax.numpy as jnp
from jax import lax
from jax.sharding import PartitionSpec as P

HD = 128
KVH = 4
GROUP = 8


epsilon = 1e-05
masked_score = -1e30


def passed_along(array, axis, by):
    peers = lax.axis_size(axis)
    pairs = [(i, i + by) for i in range(peers) if 0 <= i + by < peers]
    return lax.ppermute(array, axis, pairs)


def doc_index(position, doc_ends):
    return jnp.sum((doc_ends[None, :] <= position[:, None]).astype(jnp.int32), axis=1)


def attend_block(query_block, query_pos, query_doc, all_keys, all_values, key_pos, key_doc):
    scores = jnp.einsum(
        "qghd,kgd->ghqk", query_block, all_keys, preferred_element_type=jnp.float32
    ) / math.sqrt(HD)
    allowed = (key_pos[None, :] <= query_pos[:, None]) & (key_doc[None, :] == query_doc[:, None])
    scores = jnp.where(allowed[None, None], scores, masked_score)
    row_max = jnp.max(scores, axis=-1, keepdims=True)
    expon = jnp.exp(scores - row_max)
    weights = (expon / jnp.sum(expon, axis=-1, keepdims=True)).astype(jnp.bfloat16)
    mixed = jnp.einsum("ghqk,kgd->qghd", weights, all_values, preferred_element_type=jnp.float32)
    return mixed.astype(jnp.bfloat16)


def shards(entering, fresh_slice, norm_gain, w_query, w_key_value, doc_lengths):
    heads_here = w_query.shape[2] // HD
    slice_len = fresh_slice.shape[0]
    sections = lax.axis_size("section")
    section_index = lax.axis_index("section")
    head_index = lax.axis_index("head")
    local_groups = max(1, heads_here // GROUP)
    group_heads = heads_here // local_groups
    doc_ends = jnp.cumsum(doc_lengths)
    gain_row = norm_gain[0]
    w_q = w_query[0]
    w_kv = w_key_value[0]

    def section_layer(own_part, start, resident):
        full_rows = lax.all_gather(own_part, "head", axis=1, tiled=True)
        widened = full_rows.astype(jnp.float32)
        mean_sq = jnp.mean(widened * widened, axis=1, keepdims=True)
        normed = (widened * lax.rsqrt(mean_sq + epsilon) * gain_row[None, :]).astype(jnp.bfloat16)
        queries = jnp.dot(normed, w_q, preferred_element_type=jnp.float32).astype(jnp.bfloat16)
        kv_part = jnp.dot(normed, w_kv, preferred_element_type=jnp.float32).astype(jnp.bfloat16)
        every_column = lax.all_gather(kv_part, "head", axis=1, tiled=True)
        every_column = every_column.reshape(slice_len, HD, KVH, 2)
        first_group = head_index * heads_here // GROUP
        chosen = lax.dynamic_slice_in_dim(every_column, first_group, local_groups, 2)
        packed = jnp.transpose(chosen, (0, 2, 3, 1))
        new_keys = packed[:, :, 0, :]
        new_values = packed[:, :, 1, :]
        position = start + jnp.arange(slice_len, dtype=jnp.int32)
        if resident is None:
            all_keys, all_values, key_pos = (new_keys, new_values, position)
        else:
            all_keys = jnp.concatenate([resident[0], new_keys], axis=0)
            all_values = jnp.concatenate([resident[1], new_values], axis=0)
            key_pos = jnp.concatenate([resident[2], position], axis=0)
        key_doc = doc_index(key_pos, doc_ends)
        query_doc = doc_index(position, doc_ends)
        block_len = min(512, slice_len)
        count = slice_len // block_len
        query_groups = queries.reshape(count, block_len, local_groups, group_heads, HD)

        def one_block(block_args):
            return attend_block(
                block_args[0], block_args[1], block_args[2], all_keys, all_values, key_pos, key_doc
            )

        attended = lax.map(
            one_block,
            (query_groups, position.reshape(count, block_len), query_doc.reshape(count, block_len)),
        )
        attended = attended.reshape(slice_len, heads_here * HD)
        section_out = (own_part.astype(jnp.float32) + attended.astype(jnp.float32)).astype(
            jnp.bfloat16
        )
        return (section_out, new_keys, new_values, position)

    first_start = (sections - 1 - section_index) * slice_len
    first_out, keys_first, values_first, pos_first = section_layer(entering[0], first_start, None)
    passed = passed_along(first_out, "section", 1)
    second_in = jnp.where(section_index == 0, fresh_slice, passed)
    second_out = section_layer(
        second_in, first_start + slice_len, (keys_first, values_first, pos_first)
    )[0]
    return second_out[None]


def solution(mesh):
    placed = (
        P("section", None, "head"),
        P(None, "head"),
        P("section", None),
        P("section", None, "head"),
        P("section", None, "head"),
        P(),
    )
    return jax.shard_map(
        shards, mesh=mesh, in_specs=placed, out_specs=P("section", None, "head"), check_vma=False
    )
```

profile of v0, /device:TPU:1, one launch (start us, length us, event | category | flops | bytes accessed | tf_op | source)
XLA Modules:
  0.0 167.8 jit_solution(6120401131301652491)
XLA Ops:
  6.5 0.0 copy-start
  6.5 0.0 copy-start.6
  6.5 0.0 all-gather.6.cloned.1.call-start
  6.5 0.7 all-gather.6.cloned.1.call-update
  7.3 0.0 all-gather.4.cloned.1.call-start
  7.3 0.8 copy.29
  8.1 0.1 reduce-window.8
  8.2 0.1 reduce.4
  8.3 0.1 convert_reduce_fusion.2
  8.4 0.1 compare_and_fusion.1
  8.5 56.8 %all-gather.6.cloned.1.call-done = bf16[1,128,4096]{2,1,0:T(8,128)(2,1)} async-done(((bf16[1,128,256]{2,1,0:T(8,128)(2,1)}), bf16[1,128,4096]{2,1,0:T(8,128)(2,1)}) %all-gather.6.cloned.1.call-update) | async-done | bytes 1048592 | tf_op jit(solution)/shard_map/all_gather | solution.py:54
  65.4 0.0 copy-start.1
  65.4 1.6 fusion.3
  67.0 1.9 %convolution_convert_fusion.3 = bf16[128,64]{0,1:T(8,128)(2,1)S(1)} fusion(bf16[1,4096,64]{1,2,0:T(8,128)(2,1)} %param.10, bf16[1,128,4096]{2,1,0:T(8,128)(2,1)} %all-gather.6.cloned.1.call-done, f32[4096]{0:T(1024)} %bitcast.123, f32[128]{0:T(128)S(1)} %add_rsqrt_fusion.1), kind=kOutput, calls=%fused_computation.31 | convolution fusion | flops 69214208 | bytes 1606144 | tf_op jit(solution)/shard_map/dot_general | solution.py:59
  68.9 17.6 %all_gather.13 = bf16[128,1024]{0,1:T(8,128)(2,1)S(1)} all-gather(bf16[128,64]{0,1:T(8,128)(2,1)S(1)} %convolution_convert_fusion.3), channel_id=1, replica_groups=mesh['section'=64,'head'=16] {'head'}, dimensions={1}, use_global_device_ids=true | all-gather | bytes 278528 | tf_op jit(solution)/shard_map/all_gather | solution.py:60
  86.6 0.1 copy.45
  86.7 0.0 copy-done
  86.7 0.0 copy-done.6
  86.7 0.0 copy-done.1
  86.7 0.0 copy-start.4
  86.8 0.0 copy-start.5
  86.8 0.5 fusion.27
  87.3 0.2 fusion.57
  87.5 0.2 fusion.23
  87.7 0.1 copy.33
  87.8 0.0 copy-done.4
  87.8 3.4 %collective-permute-start = (bf16[128,256]{1,0:T(8,128)(2,1)S(1)}, bf16[128,256]{1,0:T(8,128)(2,1)S(1)}, u32[]{:S(2)}, u32[]{:S(2)}) collective-permute-start(bf16[128,256]{1,0:T(8,128)(2,1)S(1)} %fusion.37), channel_id=1, source_target_pairs={{0,16},{16,32},{32,48},{48,64},{64,80},{80,96},{96,112},{112,128},... | collective-permute-start | bytes 196616 | tf_op jit(solution)/shard_map/ppermute | solution.py:20
  91.3 1.3 collective-permute-done
  92.6 0.0 copy-done.5
  92.6 0.6 broadcast_select_fusion
  93.2 0.0 all-gather.4.cloned.1.call-update
  93.3 0.1 convert_reduce_fusion
  93.3 0.1 compare_and_fusion
  93.5 44.3 %all-gather.4.cloned.1.call-done = bf16[128,4096]{1,0:T(8,128)(2,1)} async-done(((bf16[128,256]{1,0:T(8,128)(2,1)}), bf16[128,4096]{1,0:T(8,128)(2,1)}) %all-gather.4.cloned.1.call-update) | async-done | bytes 1048592 | tf_op jit(solution)/shard_map/all_gather | solution.py:54
  137.9 0.0 copy-start.2
  137.9 1.6 fusion
  139.5 1.9 %convolution_convert_fusion.2 = bf16[128,64]{0,1:T(8,128)(2,1)S(1)} fusion(bf16[1,4096,64]{1,2,0:T(8,128)(2,1)} %param.10, bf16[128,4096]{1,0:T(8,128)(2,1)} %all-gather.4.cloned.1.call-done, f32[128]{0:T(128)S(1)} %add_rsqrt_fusion, f32[4096]{0:T(1024)S(1)} %bitcast.125), kind=kOutput, calls=%fused_computation.30 | convolution fusion | flops 69214208 | bytes 1606144 | tf_op jit(solution)/shard_map/dot_general | solution.py:59
  141.4 17.6 %all_gather.15 = bf16[128,1024]{0,1:T(8,128)(2,1)S(1)} all-gather(bf16[128,64]{0,1:T(8,128)(2,1)S(1)} %convolution_convert_fusion.2), channel_id=1, replica_groups=mesh['section'=64,'head'=16] {'head'}, dimensions={1}, use_global_device_ids=true | all-gather | bytes 278528 | tf_op jit(solution)/shard_map/all_gather | solution.py:60
  159.1 0.1 copy.46
  159.2 0.0 copy-done.2
  159.2 0.0 copy-start.3
  159.2 0.5 fusion.24
  159.7 0.2 fusion.58
  160.0 0.1 fusion.36
  160.0 0.2 fusion.21
  160.2 0.1 copy.38
  160.3 0.0 copy-done.3
  160.3 0.6 fusion.40
  (11 shorter events, 0.2 us)
Async XLA Ops:
  6.5 80.2 %copy-start = (bf16[1,4096,256]{2,1,0:T(8,128)(2,1)S(1)}, bf16[1,4096,256]{2,1,0:T(8,128)(2,1)}, u32[]{:S(2)}) copy-start(bf16[1,4096,256]{2,1,0:T(8,128)(2,1)} %param.9) | copy-start | bytes 6291460
  6.5 80.2 %copy-start.6 = (f32[1,4096]{1,0:T(1,128)S(1)}, f32[1,4096]{1,0:T(1,128)}, u32[]{:S(2)}) copy-start(f32[1,4096]{1,0:T(1,128)} %param.8) | copy-start | bytes 49156
  6.5 58.8 %all-gather.6.cloned.1.call-start = ((), (), s32[]{:S(2)}) async-start(), calls=%async_computation.1 | async-start | bytes 1114112 | tf_op jit(solution)/shard_map/all_gather | solution.py:54
  7.3 130.6 %all-gather.4.cloned.1.call-start = ((), (), s32[]{:S(2)}) async-start(), calls=%async_computation | async-start | bytes 1114112 | tf_op jit(solution)/shard_map/all_gather | solution.py:54
  65.4 21.4 %copy-start.1 = (bf16[1,128,4096]{2,1,0:T(8,128)(2,1)S(1)}, bf16[1,128,4096]{2,1,0:T(8,128)(2,1)}, u32[]{:S(2)}) copy-start(bf16[1,128,4096]{2,1,0:T(8,128)(2,1)} %all-gather.6.cloned.1.call-done) | copy-start | bytes 3145732
  86.7 1.1 copy-start.4
  86.8 5.8 %copy-start.5 = (bf16[128,256]{1,0:T(8,128)(2,1)S(1)}, bf16[128,256]{1,0:T(8,128)(2,1)}, u32[]{:S(2)}) copy-start(bf16[128,256]{1,0:T(8,128)(2,1)} %param.7) | copy-start | bytes 196612
  87.8 4.7 %collective-permute-start = (bf16[128,256]{1,0:T(8,128)(2,1)S(1)}, bf16[128,256]{1,0:T(8,128)(2,1)S(1)}, u32[]{:S(2)}, u32[]{:S(2)}) collective-permute-start(bf16[128,256]{1,0:T(8,128)(2,1)S(1)} %fusion.37), channel_id=1, source_target_pairs={{0,16},{16,32},{32,48},{48,64},{64,80},{80,96},{96,112},{112,128},... | collective-permute-start | bytes 196616 | tf_op jit(solution)/shard_map/ppermute | solution.py:20
  137.9 21.4 %copy-start.2 = (bf16[128,4096]{1,0:T(8,128)(2,1)S(1)}, bf16[128,4096]{1,0:T(8,128)(2,1)}, u32[]{:S(2)}) copy-start(bf16[128,4096]{1,0:T(8,128)(2,1)} %all-gather.4.cloned.1.call-done) | copy-start | bytes 3145732
  159.2 1.1 copy-start.3
Sparse Core Ops, SparseCore 0:
  10.0 55.3 all-gather.5
  93.4 44.4 all-gather.3
where the time goes:
time: 168 us
  waiting for transfers between devices  103 us (61%)
  blocking collectives  35.2 us (21%)
  between operations  13.7 us (8%)
  matrix products  5.62 us (3%)
  other arithmetic  5.28 us (3%)
  starting transfers between devices  3.45 us (2%)
    all_gather x2, waiting for transfers between devices, section_layer(): full_rows = lax.all_gather(own_part, 'head', axis=1, tiled=True)  101 us
    all_gather x2, blocking collectives, section_layer(): every_column = lax.all_gather(kv_part, 'head', axis=1, tiled=True)  35.2 us
    dot_general x2, matrix products, section_layer(): jnp.dot(normed, w_kv, preferred_element_type=jnp.float32)  3.84 us
    ppermute x1, starting transfers between devices, passed_along(): return lax.ppermute(array, axis, pairs)  3.41 us
  transfers between devices with their start and end apart: 3, of which 3 were waited for; matrix products, arithmetic and copies ran while one was open for 1% of the time, Pallas kernels for 0%

commit v1 on v0

v1 whole, which is shorter than its diff:
```python
import functools
import math

import jax
import jax.numpy as jnp
from jax import lax
from jax.experimental import pallas as pl
from jax.experimental.pallas import tpu as pltpu
from jax.sharding import PartitionSpec as P

MESH = pl.DeviceIdType.MESH
HD = 128
KVH = 4
GROUP = 8
EPS = 1e-05
NEG = -1e30
PIECES = 4
F32 = jnp.float32
BF16 = jnp.bfloat16
NT = (((1,), (1,)), ((), ()))


def iota(shape, dim):
    return lax.broadcasted_iota(jnp.int32, shape, dim)


def body(
    x_hbm, fresh_hbm, gain_hbm, wq_hbm, wkv_hbm, len_hbm, out_hbm,
    xg, xn, wq, wkv, wkvp, gain, lens, lens_pad, fresh, obuf, kvst, kvbuf,
    acc, sq, bias1, bias2,
    load_sem, own_sem, out_sem, ring_recv, ring_send, mate_recv, mate_send,
    hop_recv, hop_send, kv_recv, kv_send, kv_own,
):
    sections = lax.axis_size("section")
    heads = lax.axis_size("head")
    chips = heads // 2
    tokens, width = obuf.shape
    rows = tokens // PIECES
    s = lax.axis_index("section")
    h = lax.axis_index("head")
    y, core = h // 2, h % 2
    mate = (s, y * 2 + (1 - core))
    following = (s + 1) % sections
    previous = (s + sections - 1) % sections

    def chip_at(offset):
        return (y + offset + chips) % chips

    def same_core(offset):
        return chip_at(offset) * 2 + core

    def other_core(offset):
        return chip_at(offset) * 2 + 1 - core

    right, left = same_core(1), same_core(-1)

    loads = [
        pltpu.make_async_copy(src, dst, load_sem.at[i])
        for i, (src, dst) in enumerate(
            ((gain_hbm, gain), (wkv_hbm, wkv), (len_hbm, lens), (fresh_hbm, fresh), (wq_hbm, wq))
        )
    ]
    own = pltpu.make_async_copy(x_hbm, xg.at[0, h], own_sem)
    own.start()
    for load in loads:
        load.start()

    barrier = pltpu.get_barrier_semaphore()
    greeted = [(s, (h + d) % heads) for d in range(1, heads)]
    for section in (following, previous):
        for other in (h, right, left):
            greeted.append((section, other))
    for device in greeted:
        pl.semaphore_signal(barrier, inc=1, device_id=device, device_id_type=MESH)
    pl.semaphore_wait(barrier, len(greeted))

    def piece(p):
        return pl.ds(p * rows, rows)

    def send(src, dst, send_sem, recv_sem, device):
        copy = pltpu.make_async_remote_copy(
            src_ref=src, dst_ref=dst, send_sem=send_sem, recv_sem=recv_sem,
            device_id=device, device_id_type=MESH,
        )
        copy.start()
        return copy

    def await_recv(ref, sem):
        pltpu.make_async_remote_copy(
            src_ref=ref, dst_ref=ref, send_sem=sem, recv_sem=sem,
            device_id=mate, device_id_type=MESH,
        ).wait_recv()

    def await_send(ref, sem):
        pltpu.make_async_remote_copy(
            src_ref=ref, dst_ref=ref, send_sem=sem, recv_sem=sem,
            device_id=mate, device_id_type=MESH,
        ).wait_send()

    dirs = ((0, -1, (s, right)), (1, 1, (s, left)))
    half = chips // 2
    halves = (range(0, PIECES // 2), range(PIECES // 2, PIECES))

    def forward(turn, step, p, d, target):
        chunk = xg.at[turn, same_core(step if d else -step), piece(p)]
        send(chunk, chunk, ring_send.at[turn], ring_recv.at[turn, d, step, p], target)

    def to_mate(turn, offset, sel, slot):
        chunk = xg.at[turn, same_core(offset), sel]
        send(chunk, chunk, mate_send.at[turn], mate_recv.at[turn, slot], mate)

    everything = pl.ds(0, tokens)

    def first_sends():
        for p in range(PIECES):
            for d, _, target in dirs:
                send(x_hbm.at[piece(p)], xg.at[0, h, piece(p)], ring_send.at[0],
                     ring_recv.at[0, d, 0, p], target)
        send(x_hbm, xg.at[0, h], mate_send.at[0], mate_recv.at[0, 0], mate)

    def prepare():
        for load in loads[:4]:
            load.wait()
        n = wkv.shape[0]
        r, c = iota((n, n), 0), iota((n, n), 1)
        perm = (((c % 8) // 2 == r // 16) & (c // 8 == r % 8) & (c % 2 == (r % 16) // 8))
        perm = perm.astype(F32).astype(BF16)
        for j in range(heads):
            wkvp[j] = jnp.dot(
                perm, wkv[:, j * width:(j + 1) * width], preferred_element_type=F32
            ).astype(BF16)
        docs = lens.shape[1]
        lens_pad[...] = jnp.zeros_like(lens_pad)
        lens_pad[:, 0:docs] = lens[...].astype(F32)
        n = lens_pad.shape[1]
        e0, e1 = iota((n, n), 0), iota((n, n), 1)
        row = jnp.broadcast_to(lens_pad[...], (n, n))
        far = F32(1e9)
        ends_col = jnp.sum(jnp.where(e1 <= e0, row, 0.0), axis=1, keepdims=True)
        ends_col = jnp.where(iota((n, 1), 0) < docs, ends_col, far)
        ends_row = jnp.sum(jnp.where(e0 == e1, ends_col, 0.0), axis=0, keepdims=True)
        start = ((sections - 1 - s) * tokens).astype(F32)
        def docs_of_rows(begin):
            pos = begin + iota((tokens, n), 0).astype(F32)
            return jnp.sum((ends_row <= pos).astype(F32), axis=1, keepdims=True)
        def docs_of_columns(begin):
            pos = begin + iota((n, tokens), 1).astype(F32)
            return jnp.sum((ends_col <= pos).astype(F32), axis=0, keepdims=True)
        q1, q2 = docs_of_rows(start), docs_of_rows(start + tokens)
        k1, k2 = docs_of_columns(start), docs_of_columns(start + tokens)
        causal = iota((tokens, tokens), 1) <= iota((tokens, tokens), 0)
        bias1[...] = jnp.where(causal & (q1 == k1), 0.0, NEG)
        bias2[:, 0:tokens] = jnp.where(q2 == k1, 0.0, NEG)
        bias2[:, tokens:2 * tokens] = jnp.where(causal & (q2 == k2), 0.0, NEG)

    def clear():
        acc[...] = jnp.zeros_like(acc)
        sq[...] = jnp.zeros_like(sq)

    def take(turn, j):
        wide = xg[turn, j].astype(F32)
        low, high = wide[:, 0:128], wide[:, 128:256]
        sq[...] += low * low + high * high
        at = pl.multiple_of(j * width, width)
        scaled = (wide * gain[:, pl.ds(at, width)]).astype(BF16)
        xn[:, pl.ds(at, width)] = scaled
        acc[...] += lax.dot_general(wkvp[j], scaled, NT, preferred_element_type=F32)

    def take_mate(turn, offset, slot):
        await_recv(xg.at[turn, 0], mate_recv.at[turn, slot])
        take(turn, other_core(offset))

    group = h * (width // HD) // GROUP
    sel_r, sel_c = iota((HD, 2 * HD), 0), iota((HD, 2 * HD), 1)
    same_peer = sel_r // 8 == sel_c // 16
    pick_key = (same_peer & (sel_c % 16 == sel_r % 8)).astype(F32).astype(BF16)
    pick_value = (same_peer & (sel_c % 16 == 8 + sel_r % 8)).astype(F32).astype(BF16)

    def exchange(turn):
        mean_sq = jnp.sum(sq[...], axis=1, keepdims=True) * (1.0 / (heads * width))
        scale = lax.rsqrt(mean_sq + EPS)
        diag = iota((tokens, tokens), 0) == iota((tokens, tokens), 1)
        scale_row = jnp.sum(jnp.where(diag, scale, 0.0), axis=0, keepdims=True)
        kvst[turn] = (acc[...] * scale_row).astype(BF16).reshape(KVH, 16, tokens)
        for d in range(1, heads):
            peer = (h + d) % heads
            send(kvst.at[turn, peer * (width // HD) // GROUP], kvbuf.at[turn, h],
                 kv_send.at[turn], kv_recv.at[turn], (s, peer))
        keep = pltpu.make_async_copy(kvst.at[turn, group], kvbuf.at[turn, h], kv_own.at[turn])
        keep.start()
        return scale, keep

    def queries(scale):
        q = jnp.dot(xn[...], wq[...], preferred_element_type=F32)
        q = (q * scale).astype(BF16)
        spread = [
            jnp.dot(q[:, i * HD:(i + 1) * HD], pick_key, preferred_element_type=F32)
            for i in range(width // HD)
        ]
        return jnp.concatenate(spread, axis=0).astype(BF16)

    def await_kv(turn, keep):
        keep.wait()
        await_recv(kvbuf.at[turn, pl.ds(0, heads - 1)], kv_recv.at[turn])

    def attend(turn, wide_q, bias):
        here = width // HD
        turns = range(turn + 1)
        both = [kvbuf[t].reshape(heads * 16, tokens) for t in turns]
        scores = [
            jnp.dot(wide_q, kv, preferred_element_type=F32) * (1.0 / math.sqrt(HD)) for kv in both
        ]
        scores = jnp.concatenate(scores, axis=1) + jnp.concatenate([bias[...]] * here, axis=0)
        expon = jnp.exp(scores - jnp.max(scores, axis=1, keepdims=True))
        weights = (expon / jnp.sum(expon, axis=1, keepdims=True)).astype(BF16)
        values = [
            jnp.dot(pick_value, kv, preferred_element_type=F32).astype(BF16) for kv in both
        ]
        values = jnp.concatenate(values, axis=1)
        mixed = lax.dot_general(weights, values, NT, preferred_element_type=F32).astype(BF16)
        for i in range(here):
            cols = slice(i * HD, (i + 1) * HD)
            total = xg[turn, h, :, cols].astype(F32) + mixed[i * tokens:(i + 1) * tokens].astype(F32)
            if turn == 0:
                total = jnp.where(s == sections - 1, fresh[:, cols].astype(F32), total)
            obuf[:, cols] = total.astype(BF16)

    def rest_of_ring(turn, step):
        for p in range(PIECES):
            for d, sign, target in dirs:
                if step == half and p not in halves[d]:
                    continue
                chunk = xg.at[turn, same_core(sign * step), piece(p)]
                await_recv(chunk, ring_recv.at[turn, d, step - 1, p])
                if step < half - 1 or (step == half - 1 and p in halves[d]):
                    forward(turn, step, p, d, target)
                slot = 2 * step - 1 + (d if step < half else 0)
                to_mate(turn, sign * step, piece(p), slot)

    def take_step(turn, step):
        take(turn, same_core(-step))
        if step < half:
            take(turn, same_core(step))
        take_mate(turn, -step, 2 * step - 1)
        if step < half:
            take_mate(turn, step, 2 * step)

    first_sends()
    clear()
    prepare()
    own.wait()
    take(0, h)
    take_mate(0, 0, 0)
    for step in range(1, half + 1):
        rest_of_ring(0, step)
        if step > 1:
            take_step(0, step - 1)
    take_step(0, half)
    scale, keep = exchange(0)
    loads[4].wait()
    wide_q = queries(scale)
    await_kv(0, keep)
    attend(0, wide_q, bias1)

    for p in range(PIECES):
        for slot, other in ((0, h), (1, right), (2, left)):
            send(obuf.at[piece(p)], xg.at[1, h, piece(p)], hop_send,
                 hop_recv.at[p] if slot == 0 else ring_recv.at[1, slot - 1, 0, p],
                 (following, other))

    clear()
    for p in range(PIECES):
        await_recv(xg.at[1, h, piece(p)], hop_recv.at[p])
        to_mate(1, 0, piece(p), 0)
    for step in range(1, half + 1):
        rest_of_ring(1, step)
        if step == 1:
            take(1, h)
            take_mate(1, 0, 0)
        else:
            take_step(1, step - 1)
    take_step(1, half)
    scale, keep = exchange(1)
    wide_q = queries(scale)
    await_kv(1, keep)
    for _ in range(3):
        pass
    await_send(xg.at[0, pl.ds(0, 3)], hop_send)
    attend(1, wide_q, bias2)
    result = pltpu.make_async_copy(obuf, out_hbm, out_sem)
    result.start()

    await_send(xg.at[0, pl.ds(0, 2 * half - 1)], ring_send.at[0])
    await_send(xg.at[1, pl.ds(0, 2 * half - 3)], ring_send.at[1])
    for turn in range(2):
        await_send(xg.at[turn, pl.ds(0, 2 * half)], mate_send.at[turn])
        await_send(kvbuf.at[turn, pl.ds(0, heads - 1)], kv_send.at[turn])
    result.wait()


def solution(mesh):
    heads = mesh.shape["head"]
    half = heads // 4

    def shards(entering, fresh_slice, norm_gain, w_query, w_key_value, doc_lengths):
        _, tokens, width = entering.shape
        features = w_query.shape[1]
        columns = w_key_value.shape[2]
        docs = doc_lengths.shape[0]
        any_spec = pl.BlockSpec(memory_space=pl.ANY)
        dma = pltpu.SemaphoreType.DMA
        out = pl.pallas_call(
            body,
            out_shape=jax.ShapeDtypeStruct((tokens, width), BF16),
            in_specs=[any_spec] * 6,
            out_specs=any_spec,
            scratch_shapes=[
                pltpu.VMEM((2, heads, tokens, width), BF16),
                pltpu.VMEM((tokens, features), BF16),
                pltpu.VMEM((features, width), BF16),
                pltpu.VMEM((columns, features), BF16),
                pltpu.VMEM((heads, columns, width), BF16),
                pltpu.VMEM((1, features), F32),
                pltpu.VMEM((1, docs), jnp.int32),
                pltpu.VMEM((1, 128), F32),
                pltpu.VMEM((tokens, width), BF16),
                pltpu.VMEM((tokens, width), BF16),
                pltpu.VMEM((2, KVH, 16, tokens), BF16),
                pltpu.VMEM((2, heads, 16, tokens), BF16),
                pltpu.VMEM((columns, tokens), F32),
                pltpu.VMEM((tokens, 128), F32),
                pltpu.VMEM((tokens, tokens), F32),
                pltpu.VMEM((tokens, 2 * tokens), F32),
                dma((5,)),
                dma,
                dma,
                dma((2, 2, half, PIECES)),
                dma((2,)),
                dma((2, 2 * half)),
                dma((2,)),
                dma((PIECES,)),
                dma,
                dma((2,)),
                dma((2,)),
                dma((2,)),
            ],
            compiler_params=pltpu.CompilerParams(collective_id=0, has_side_effects=True),
        )(
            entering[0], fresh_slice, norm_gain, w_query[0], w_key_value[0].T,
            doc_lengths.reshape(1, docs),
        )
        return out[None]

    placed = (
        P("section", None, "head"),
        P(None, "head"),
        P("section", None),
        P("section", None, "head"),
        P("section", None, "head"),
        P(),
    )
    return jax.shard_map(
        shards, mesh=mesh, in_specs=placed, out_specs=P("section", None, "head"), check_vma=False
    )
```

time: 168 us -> 69.9 us (0.42)
  waiting for transfers between devices: 103 us -> 0 us
  Pallas kernels: 0 us -> 68.3 us
  blocking collectives: 35.2 us -> 0 us
  between operations: 13.7 us -> 0.01 us
  matrix products: 5.62 us -> 0 us
  other arithmetic: 5.28 us -> 0 us
  starting transfers between devices: 3.45 us -> 0 us
    all_gather x2 -> x0, waiting for transfers between devices: 101 us -> none  [section_layer(): full_rows = lax.all_gather(own_part, 'head', axis=1, tiled=True)]
    pallas_call x0 -> x1, Pallas kernels: none -> 68.3 us  [shards(): pl.pallas_call(body, out_shape=jax.ShapeDtypeStruct((tokens, width), BF16...]
    all_gather x2 -> x0, blocking collectives: 35.2 us -> none  [section_layer(): every_column = lax.all_gather(kv_part, 'head', axis=1, tiled=True)]
    dot_general x8 -> x0, matrix products: 5.62 us -> none  [the longest x2 3.84 us: section_layer(): jnp.dot(normed, w_kv, preferred_element_type=jnp.float32)]
    reduce_sum x6 -> x0, other arithmetic: 3.5 us -> none  [the longest x2 3.21 us: section_layer(): mean_sq = jnp.mean(widened * widened, axis=1, keepdims=True)]
    ppermute x1 -> x0, starting transfers between devices: 3.41 us -> none  [passed_along(): return lax.ppermute(array, axis, pairs)]
  transfers between devices with their start and end apart: 3 -> 0, of which waited for: 3 -> 0; matrix products, arithmetic and copies ran while one was open for 1% -> 0% of each run, Pallas kernels for 0% -> 0%
where the time goes in v1:
time: 69.9 us; the launch traced here: 69.7 us
  Pallas kernels  68.3 us (98%)
  local copies, waits for them, and re-layouts  1.47 us (2%)
    pallas_call x1, Pallas kernels, shards(): pl.pallas_call(body, out_shape=jax.ShapeDtypeStruct((tokens, width), BF16...  68.3 us
    unnamed x1, local copies, waits for them, and re-layouts  1.47 us

profile of v1, /device:TPU:1, one launch (start us, length us, event | category | flops | bytes accessed | tf_op | source)
XLA Modules:
  0.0 69.7 jit_solution(879346529418669402)
XLA Ops:
  0.0 68.3 %shard_map.64 = bf16[128,256]{1,0:T(8,128)(2,1)} custom-call(bf16[128,256]{1,0:T(8,128)(2,1)} %bitcast.10, bf16[128,256]{1,0:T(8,128)(2,1)} %fresh_hbm.1, f32[1,4096]{1,0:T(1,128)} %gain_hbm.1, bf16[4096,256]{1,0:T(8,128)(2,1)} %bitcast.7, bf16[64,4096]{1,0:T(8,128)(2,1)} %bitcast.8, s32[1,65]{1,0:T(1,128)} %bitcast.11), custom_call_target="tpu_custom_call" | custom-call | tf_op jit(solution)/shard_map/pallas_call | solution.py:312
  68.3 1.5 %copy.8 = bf16[1,128,256]{2,1,0:T(8,128)(2,1)} copy(bf16[1,128,256]{2,1,0:T(8,128)(2,1)} %bitcast.9) | data formatting | bytes 131072

commit v2 on v1

--- a/solution.py
+++ b/solution.py
@@ -66,13 +66,10 @@
         load.start()
 
     barrier = pltpu.get_barrier_semaphore()
-    greeted = [(s, (h + d) % heads) for d in range(1, heads)]
-    for section in (following, previous):
-        for other in (h, right, left):
-            greeted.append((section, other))
-    for device in greeted:
+    near = (h, right, left)
+    for device in [mate, (s, right), (s, left)] + [(previous, other) for other in near]:
         pl.semaphore_signal(barrier, inc=1, device_id=device, device_id_type=MESH)
-    pl.semaphore_wait(barrier, len(greeted))
+    pl.semaphore_wait(barrier, 6)
 
     def piece(p):
         return pl.ds(p * rows, rows)
@@ -283,8 +280,6 @@
     scale, keep = exchange(1)
     wide_q = queries(scale)
     await_kv(1, keep)
-    for _ in range(3):
-        pass
     await_send(xg.at[0, pl.ds(0, 3)], hop_send)
     attend(1, wide_q, bias2)
     result = pltpu.make_async_copy(obuf, out_hbm, out_sem)

time: 69.9 us -> 69 us (0.987)
  Pallas kernels: 68.3 us -> 67.3 us
    pallas_call x1, Pallas kernels: 68.3 us -> 67.3 us  [shards(): pl.pallas_call(body, out_shape=jax.ShapeDtypeStruct((tokens, width), BF16...]
where the time goes in v2:
time: 69 us; the launch traced here: 68.8 us
  Pallas kernels  67.3 us (98%)
  local copies, waits for them, and re-layouts  1.47 us (2%)
    pallas_call x1, Pallas kernels, shards(): pl.pallas_call(body, out_shape=jax.ShapeDtypeStruct((tokens, width), BF16...  67.3 us
    unnamed x1, local copies, waits for them, and re-layouts  1.47 us

profile of v2, /device:TPU:1, one launch (start us, length us, event | category | flops | bytes accessed | tf_op | source)
XLA Modules:
  0.0 68.8 jit_solution(5475007921073880162)
XLA Ops:
  0.0 67.3 %shard_map.64 = bf16[128,256]{1,0:T(8,128)(2,1)} custom-call(bf16[128,256]{1,0:T(8,128)(2,1)} %bitcast.10, bf16[128,256]{1,0:T(8,128)(2,1)} %fresh_hbm.1, f32[1,4096]{1,0:T(1,128)} %gain_hbm.1, bf16[4096,256]{1,0:T(8,128)(2,1)} %bitcast.7, bf16[64,4096]{1,0:T(8,128)(2,1)} %bitcast.8, s32[1,65]{1,0:T(1,128)} %bitcast.11), custom_call_target="tpu_custom_call" | custom-call | tf_op jit(solution)/shard_map/pallas_call | solution.py:307
  67.3 1.5 %copy.8 = bf16[1,128,256]{2,1,0:T(8,128)(2,1)} copy(bf16[1,128,256]{2,1,0:T(8,128)(2,1)} %bitcast.9) | data formatting | bytes 131072

commit v3 on v2

v3 whole, which is shorter than its diff:
```python
import functools
import math

import jax
import jax.numpy as jnp
from jax import lax
from jax.experimental import pallas as pl
from jax.experimental.pallas import tpu as pltpu
from jax.sharding import PartitionSpec as P

MESH = pl.DeviceIdType.MESH
HD = 128
KVH = 4
GROUP = 8
EPS = 1e-05
NEG = -1e30
PIECES = 4
F32 = jnp.float32
BF16 = jnp.bfloat16
NT = (((1,), (1,)), ((), ()))


def iota(shape, dim):
    return lax.broadcasted_iota(jnp.int32, shape, dim)


def body(
    x_hbm, fresh_hbm, gain_hbm, wq_hbm, wkv_hbm, len_hbm, out_ref,
    xg, xn, wq, wkv_raw, wkv, gain, lens, lens_pad, fresh, first, kvst, kvbuf,
    acc, sq, part_out, part_in, query_out, query_in, bias1, bias2,
    load_sem, own_sem, swap_send, swap_recv, ring_recv, ring_send, hop_send,
    part_send, part_recv, query_send, query_recv, kv_recv, kv_send, kv_own,
):
    sections = lax.axis_size("section")
    heads = lax.axis_size("head")
    chips = heads // 2
    tokens, width = first.shape
    columns = wkv_hbm.shape[0]
    rows = tokens // PIECES
    here = width // HD
    s = lax.axis_index("section")
    h = lax.axis_index("head")
    y, core = h // 2, h % 2
    mate = (s, y * 2 + (1 - core))
    following = ((s + 1) % sections, h)
    previous = ((s + sections - 1) % sections, h)

    def chip(offset):
        return (y + offset + chips) % chips

    def peer(offset):
        return (s, chip(offset) * 2 + core)

    def send(src, dst, send_sem, recv_sem, device):
        pltpu.make_async_remote_copy(
            src_ref=src, dst_ref=dst, send_sem=send_sem, recv_sem=recv_sem,
            device_id=device, device_id_type=MESH,
        ).start()

    def await_recv(ref, sem):
        pltpu.make_async_remote_copy(
            src_ref=ref, dst_ref=ref, send_sem=sem, recv_sem=sem,
            device_id=mate, device_id_type=MESH,
        ).wait_recv()

    def await_send(ref, sem):
        pltpu.make_async_remote_copy(
            src_ref=ref, dst_ref=ref, send_sem=sem, recv_sem=sem,
            device_id=mate, device_id_type=MESH,
        ).wait_send()

    def piece(p):
        return pl.ds(p * rows, rows)

    barrier = pltpu.get_barrier_semaphore()
    greeted = [mate, peer(1), peer(-1), peer(2), peer(-2), previous]
    for device in greeted:
        pl.semaphore_signal(barrier, inc=1, device_id=device, device_id_type=MESH)

    own = pltpu.make_async_copy(x_hbm, xg.at[0, y], own_sem)
    own.start()
    loads = [
        pltpu.make_async_copy(src, dst, load_sem.at[i])
        for i, (src, dst) in enumerate(
            ((gain_hbm, gain), (len_hbm, lens), (fresh_hbm, fresh), (wq_hbm.at[:, core], wq.at[0]))
        )
    ]
    for load in loads:
        load.start()

    def lanes(k, parity):
        return pl.ds(pl.multiple_of((2 * k + parity) * width, width), width)

    for k in range(chips):
        pltpu.make_async_copy(
            wkv_hbm.at[:, lanes(k, core)], wkv_raw.at[0, k], load_sem.at[4]
        ).start()
    pl.semaphore_wait(barrier, len(greeted))

    half = chips // 2
    halves = (range(0, PIECES // 2), range(PIECES // 2, PIECES))
    sides = ((0, 1), (1, -1))
    passed_by = {1: 0, 2: 0, 3: 2, 4: 2}

    def pieces(k, d):
        return range(PIECES) if k < half else halves[d]

    def pass_on(turn, k, p, d, src=None):
        sign = sides[d][1]
        owner = chip(-sign * k)
        chunk = xg.at[turn, owner, piece(p)]
        for k2 in (4, 3, 2, 1):
            if passed_by[k2] == k and k2 > k and p in pieces(k2, d):
                send(chunk if src is None else src, chunk, ring_send.at[turn],
                     ring_recv.at[turn, d, k2, p], peer(sign * (k2 - k)))

    def await_ring(turn, k):
        for p in range(PIECES):
            for d, sign in sides:
                if p in pieces(k, d):
                    await_recv(xg.at[turn, chip(-sign * k), piece(p)], ring_recv.at[turn, d, k, p])
                    pass_on(turn, k, p, d)

    def swap_weights():
        for k in range(chips):
            send(wkv_hbm.at[:, lanes(k, 1 - core)], wkv_raw.at[1, k], swap_send.at[0],
                 swap_recv.at[0], mate)
        send(wq_hbm.at[:, 1 - core], wq.at[1], swap_send.at[1], swap_recv.at[1], mate)

    def prepare():
        for load in loads[:3]:
            load.wait()
        docs = lens.shape[1]
        lens_pad[...] = jnp.zeros_like(lens_pad)
        lens_pad[:, 0:docs] = lens[...].astype(F32)
        n = lens_pad.shape[1]
        e0, e1 = iota((n, n), 0), iota((n, n), 1)
        row = jnp.broadcast_to(lens_pad[...], (n, n))
        far = F32(1e9)
        ends_col = jnp.sum(jnp.where(e1 <= e0, row, 0.0), axis=1, keepdims=True)
        ends_col = jnp.where(iota((n, 1), 0) < docs, ends_col, far)
        ends_row = jnp.sum(jnp.where(e0 == e1, ends_col, 0.0), axis=0, keepdims=True)
        start = ((sections - 1 - s) * tokens).astype(F32)

        def docs_of_rows(begin):
            pos = begin + iota((tokens, n), 0).astype(F32)
            return jnp.sum((ends_row <= pos).astype(F32), axis=1, keepdims=True)

        def docs_of_columns(begin):
            pos = begin + iota((n, tokens), 1).astype(F32)
            return jnp.sum((ends_col <= pos).astype(F32), axis=0, keepdims=True)

        q1, q2 = docs_of_rows(start), docs_of_rows(start + tokens)
        k1, k2 = docs_of_columns(start), docs_of_columns(start + tokens)
        causal = iota((tokens, tokens), 1) <= iota((tokens, tokens), 0)
        bias1[...] = jnp.where(causal & (q1 == k1), 0.0, NEG)
        bias2[:, 0:tokens] = jnp.where(q2 == k1, 0.0, NEG)
        bias2[:, tokens:2 * tokens] = jnp.where(causal & (q2 == k2), 0.0, NEG)
        r, c = iota((columns, columns), 0), iota((columns, columns), 1)
        perm = (((c % 8) // 2 == r // 16) & (c // 8 == r % 8) & (c % 2 == (r % 16) // 8))
        perm = perm.astype(F32).astype(BF16)
        pltpu.make_async_copy(wkv_raw.at[0], wkv_raw.at[0], load_sem.at[4]).wait()
        await_recv(wkv_raw.at[1], swap_recv.at[0])
        for k in range(chips):
            for side in range(2):
                wkv[k, side * columns:(side + 1) * columns] = jnp.dot(
                    perm, wkv_raw[side, k], preferred_element_type=F32
                ).astype(BF16)

    def clear():
        acc[...] = jnp.zeros_like(acc)
        sq[...] = jnp.zeros_like(sq)

    def take(turn, offset):
        k = chip(offset)
        wide = xg[turn, k].astype(F32)
        low, high = wide[:, 0:128], wide[:, 128:256]
        sq[...] += low * low + high * high
        scaled = (wide * gain[:, lanes(k, core)]).astype(BF16)
        xn[:, pl.ds(pl.multiple_of(k * width, width), width)] = scaled
        acc[...] += lax.dot_general(wkv[k], scaled, NT, preferred_element_type=F32)

    def take_both(turn, k):
        take(turn, -k)
        if k < half:
            take(turn, k)

    group = h * here // GROUP
    sel_r, sel_c = iota((HD, 2 * HD), 0), iota((HD, 2 * HD), 1)
    same_peer = sel_r // 8 == sel_c // 16
    pick_key = (same_peer & (sel_c % 16 == sel_r % 8)).astype(F32).astype(BF16)
    pick_value = (same_peer & (sel_c % 16 == 8 + sel_r % 8)).astype(F32).astype(BF16)
    diag = iota((tokens, tokens), 0) == iota((tokens, tokens), 1)

    def exchange(turn):
        square = jnp.sum(sq[...], axis=1, keepdims=True)
        square = jnp.sum(jnp.where(diag, square, 0.0), axis=0, keepdims=True)
        part_out[turn, 0:columns] = acc[columns:2 * columns]
        part_out[turn, columns:columns + 8] = jnp.broadcast_to(square, (8, tokens))
        send(part_out.at[turn], part_in.at[turn], part_send.at[turn], part_recv.at[turn], mate)
        await_recv(part_in.at[turn], part_recv.at[turn])
        square = square + part_in[turn, columns:columns + 1]
        scale = lax.rsqrt(square * (1.0 / (heads * width)) + EPS)
        total = acc[0:columns] + part_in[turn, 0:columns]
        kvst[turn] = (total * scale).astype(BF16).reshape(KVH, 16, tokens)
        for d in range(1, heads):
            other = (h + d) % heads
            send(kvst.at[turn, other * here // GROUP], kvbuf.at[turn, h],
                 kv_send.at[turn], kv_recv.at[turn], (s, other))
        keep = pltpu.make_async_copy(kvst.at[turn, group], kvbuf.at[turn, h], kv_own.at[turn])
        keep.start()
        return scale, keep

    def queries(turn, scale):
        def product(side):
            w = wq[side].reshape(chips * width, width)
            return jnp.dot(xn[...], w, preferred_element_type=F32)

        query_out[turn] = product(1)
        send(query_out.at[turn], query_in.at[turn], query_send.at[turn], query_recv.at[turn], mate)
        q = product(0)
        scale = jnp.sum(jnp.where(diag, scale, 0.0), axis=1, keepdims=True)
        await_recv(query_in.at[turn], query_recv.at[turn])
        q = ((q + query_in[turn]) * scale).astype(BF16)
        spread = [
            jnp.dot(q[:, i * HD:(i + 1) * HD], pick_key, preferred_element_type=F32)
            for i in range(here)
        ]
        return jnp.concatenate(spread, axis=0).astype(BF16)

    def await_kv(turn, keep):
        keep.wait()
        await_recv(kvbuf.at[turn, pl.ds(0, heads - 1)], kv_recv.at[turn])

    def attend(turn, wide_q, bias):
        both = [kvbuf[t].reshape(heads * 16, tokens) for t in range(turn + 1)]
        scores = [
            jnp.dot(wide_q, kv, preferred_element_type=F32) * (1.0 / math.sqrt(HD)) for kv in both
        ]
        scores = jnp.concatenate(scores, axis=1) + jnp.concatenate([bias[...]] * here, axis=0)
        expon = jnp.exp(scores - jnp.max(scores, axis=1, keepdims=True))
        weights = (expon / jnp.sum(expon, axis=1, keepdims=True)).astype(BF16)
        values = [
            jnp.dot(pick_value, kv, preferred_element_type=F32).astype(BF16) for kv in both
        ]
        values = jnp.concatenate(values, axis=1)
        mixed = lax.dot_general(weights, values, NT, preferred_element_type=F32).astype(BF16)
        mixed = mixed.astype(F32)
        for i in range(here):
            cols = slice(i * HD, (i + 1) * HD)
            total = xg[turn, y, :, cols].astype(F32) + mixed[i * tokens:(i + 1) * tokens]
            if turn == 0:
                total = jnp.where(s == sections - 1, fresh[:, cols].astype(F32), total)
                first[:, cols] = total.astype(BF16)
            else:
                out_ref[:, cols] = total.astype(BF16)

    def rest_of_gather(turn):
        await_ring(turn, 2)
        take(turn, 0)
        await_ring(turn, 1)
        take_both(turn, 1)
        take_both(turn, 2)
        await_ring(turn, 3)
        take_both(turn, 3)
        await_ring(turn, 4)
        take_both(turn, 4)

    for p in range(PIECES):
        for d, _ in sides:
            pass_on(0, 0, p, d, x_hbm.at[piece(p)])
    swap_weights()
    clear()
    prepare()
    own.wait()
    rest_of_gather(0)
    scale, keep = exchange(0)
    loads[3].wait()
    await_recv(wq.at[1], swap_recv.at[1])
    wide_q = queries(0, scale)
    await_kv(0, keep)
    attend(0, wide_q, bias1)

    for p in range(PIECES):
        send(first.at[piece(p)], xg.at[1, y, piece(p)], hop_send, ring_recv.at[1, 0, 0, p], following)

    clear()
    for p in range(PIECES):
        await_recv(xg.at[1, y, piece(p)], ring_recv.at[1, 0, 0, p])
        for d, _ in sides:
            pass_on(1, 0, p, d)
    rest_of_gather(1)
    scale, keep = exchange(1)
    wide_q = queries(1, scale)
    await_kv(1, keep)
    attend(1, wide_q, bias2)

    await_send(first, hop_send)
    await_send(wkv_raw.at[1], swap_send.at[0])
    await_send(wq.at[1], swap_send.at[1])
    for turn in range(2):
        await_send(xg.at[turn, pl.ds(0, 2 * half - 1)], ring_send.at[turn])
        await_send(part_out.at[turn], part_send.at[turn])
        await_send(query_out.at[turn], query_send.at[turn])
        await_send(kvbuf.at[turn, pl.ds(0, heads - 1)], kv_send.at[turn])


def solution(mesh):
    heads = mesh.shape["head"]
    chips = heads // 2

    def shards(entering, fresh_slice, norm_gain, w_query, w_key_value, doc_lengths):
        _, tokens, width = entering.shape
        features = w_query.shape[1]
        columns = w_key_value.shape[2]
        docs = doc_lengths.shape[0]
        any_spec = pl.BlockSpec(memory_space=pl.ANY)
        dma = pltpu.SemaphoreType.DMA
        vmem = pltpu.VMEM
        out = pl.pallas_call(
            body,
            out_shape=jax.ShapeDtypeStruct((tokens, width), BF16),
            in_specs=[any_spec] * 6,
            out_specs=pl.BlockSpec(memory_space=pltpu.VMEM),
            scratch_shapes=[
                vmem((2, chips, tokens, width), BF16),
                vmem((tokens, features // 2), BF16),
                vmem((2, chips, width, width), BF16),
                vmem((2, chips, columns, width), BF16),
                vmem((chips, 2 * columns, width), BF16),
                vmem((1, features), F32),
                vmem((1, docs), jnp.int32),
                vmem((1, 128), F32),
                vmem((tokens, width), BF16),
                vmem((tokens, width), BF16),
                vmem((2, KVH, 16, tokens), BF16),
                vmem((2, heads, 16, tokens), BF16),
                vmem((2 * columns, tokens), F32),
                vmem((tokens, 128), F32),
                vmem((2, columns + 8, tokens), F32),
                vmem((2, columns + 8, tokens), F32),
                vmem((2, tokens, width), F32),
                vmem((2, tokens, width), F32),
                vmem((tokens, tokens), F32),
                vmem((tokens, 2 * tokens), F32),
                dma((5,)),
                dma,
                dma((2,)),
                dma((2,)),
                dma((2, 2, 5, PIECES)),
                dma((2,)),
                dma,
                dma((2,)),
                dma((2,)),
                dma((2,)),
                dma((2,)),
                dma((2,)),
                dma((2,)),
                dma((2,)),
            ],
            compiler_params=pltpu.CompilerParams(collective_id=0, has_side_effects=True),
        )(
            entering[0], fresh_slice, norm_gain, w_query[0].reshape(chips, 2, width, width),
            w_key_value[0].T, doc_lengths.reshape(1, docs),
        )
        return out[None]

    placed = (
        P("section", None, "head"),
        P(None, "head"),
        P("section", None),
        P("section", None, "head"),
        P("section", None, "head"),
        P(),
    )
    return jax.shard_map(
        shards, mesh=mesh, in_specs=placed, out_specs=P("section", None, "head"), check_vma=False
    )
```

time: 69 us -> 64.2 us (0.930)
  Pallas kernels: 67.3 us -> 62.5 us
    pallas_call x1, Pallas kernels: 67.3 us -> 62.5 us  [shards(): pl.pallas_call(body, out_shape=jax.ShapeDtypeStruct((tokens, width), BF16...]
where the time goes in v3:
time: 64.2 us; the launch traced here: 63.9 us
  Pallas kernels  62.5 us (97%)
  local copies, waits for them, and re-layouts  1.47 us (2%)
    pallas_call x1, Pallas kernels, shards(): pl.pallas_call(body, out_shape=jax.ShapeDtypeStruct((tokens, width), BF16...  62.5 us
    unnamed x1, local copies, waits for them, and re-layouts  1.47 us

profile of v3, /device:TPU:1, one launch (start us, length us, event | category | flops | bytes accessed | tf_op | source)
XLA Modules:
  0.0 63.9 jit_solution(11438728618128633298)
XLA Ops:
  0.0 62.5 %shard_map.64 = bf16[128,256]{1,0:T(8,128)(2,1)} custom-call(bf16[128,256]{1,0:T(8,128)(2,1)} %bitcast.10, bf16[128,256]{1,0:T(8,128)(2,1)} %fresh_hbm.1, f32[1,4096]{1,0:T(1,128)} %gain_hbm.1, bf16[8,2,256,256]{3,2,1,0:T(8,128)(2,1)} %bitcast.7, bf16[64,4096]{1,0:T(8,128)(2,1)} %bitcast.8, s32[1,65]{1,0:T(1,128)} %bitcast.11), custom_call_target="tpu_custom_call" | custom-call | tf_op jit(solution)/shard_map/pallas_call | solution.py:320
  62.5 1.5 %copy.8 = bf16[1,128,256]{2,1,0:T(8,128)(2,1)} copy(bf16[1,128,256]{2,1,0:T(8,128)(2,1)} %bitcast.9) | data formatting | bytes 131072

commit v4 on v3

--- a/solution.py
+++ b/solution.py
@@ -127,8 +127,8 @@
                  swap_recv.at[0], mate)
         send(wq_hbm.at[:, 1 - core], wq.at[1], swap_send.at[1], swap_recv.at[1], mate)
 
-    def prepare():
-        for load in loads[:3]:
+    def masks():
+        for load in loads[1:3]:
             load.wait()
         docs = lens.shape[1]
         lens_pad[...] = jnp.zeros_like(lens_pad)
@@ -156,9 +156,11 @@
         bias1[...] = jnp.where(causal & (q1 == k1), 0.0, NEG)
         bias2[:, 0:tokens] = jnp.where(q2 == k1, 0.0, NEG)
         bias2[:, tokens:2 * tokens] = jnp.where(causal & (q2 == k2), 0.0, NEG)
+    def order_columns():
         r, c = iota((columns, columns), 0), iota((columns, columns), 1)
         perm = (((c % 8) // 2 == r // 16) & (c // 8 == r % 8) & (c % 2 == (r % 16) // 8))
         perm = perm.astype(F32).astype(BF16)
+        loads[0].wait()
         pltpu.make_async_copy(wkv_raw.at[0], wkv_raw.at[0], load_sem.at[4]).wait()
         await_recv(wkv_raw.at[1], swap_recv.at[0])
         for k in range(chips):
@@ -203,8 +205,9 @@
         scale = lax.rsqrt(square * (1.0 / (heads * width)) + EPS)
         total = acc[0:columns] + part_in[turn, 0:columns]
         kvst[turn] = (total * scale).astype(BF16).reshape(KVH, 16, tokens)
-        for d in range(1, heads):
-            other = (h + d) % heads
+        far_first = sorted(range(1 - half, half + 1), key=abs, reverse=True)
+        others = [chip(far) * 2 + side for far in far_first if far for side in (core, 1 - core)]
+        for other in others + [y * 2 + 1 - core]:
             send(kvst.at[turn, other * here // GROUP], kvbuf.at[turn, h],
                  kv_send.at[turn], kv_recv.at[turn], (s, other))
         keep = pltpu.make_async_copy(kvst.at[turn, group], kvbuf.at[turn, h], kv_own.at[turn])
@@ -257,6 +260,9 @@
 
     def rest_of_gather(turn):
         await_ring(turn, 2)
+        if turn == 0:
+            order_columns()
+            own.wait()
         take(turn, 0)
         await_ring(turn, 1)
         take_both(turn, 1)
@@ -271,13 +277,12 @@
             pass_on(0, 0, p, d, x_hbm.at[piece(p)])
     swap_weights()
     clear()
-    prepare()
-    own.wait()
     rest_of_gather(0)
     scale, keep = exchange(0)
     loads[3].wait()
     await_recv(wq.at[1], swap_recv.at[1])
     wide_q = queries(0, scale)
+    masks()
     await_kv(0, keep)
     attend(0, wide_q, bias1)
 
@@ -319,7 +324,7 @@
         vmem = pltpu.VMEM
         out = pl.pallas_call(
             body,
-            out_shape=jax.ShapeDtypeStruct((tokens, width), BF16),
+            out_shape=pltpu.VMEM((tokens, width), BF16),
             in_specs=[any_spec] * 6,
             out_specs=pl.BlockSpec(memory_space=pltpu.VMEM),
             scratch_shapes=[

time: 64.2 us -> 62 us (0.966)
  Pallas kernels: 62.5 us -> 61.2 us
  local copies, waits for them, and re-layouts: 1.47 us -> 0.63 us
    pallas_call x1, Pallas kernels: 62.5 us -> 61.2 us  [shards(): pl.pallas_call(body, out_shape=pltpu.VMEM((tokens, width), BF16), in_spec...]
    unnamed x1, local copies, waits for them, and re-layouts: 1.47 us -> 0.63 us
where the time goes in v4:
time: 62 us; the launch traced here: 61.8 us
  Pallas kernels  61.2 us (99%)
  local copies, waits for them, and re-layouts  0.63 us (1%)
    pallas_call x1, Pallas kernels, shards(): pl.pallas_call(body, out_shape=pltpu.VMEM((tokens, width), BF16), in_spec...  61.2 us

profile of v4, /device:TPU:1, one launch (start us, length us, event | category | flops | bytes accessed | tf_op | source)
XLA Modules:
  0.0 61.8 jit_solution(2140422769831007099)
XLA Ops:
  0.0 61.2 %shard_map.64 = bf16[128,256]{1,0:T(8,128)(2,1)S(1)} custom-call(bf16[128,256]{1,0:T(8,128)(2,1)} %bitcast.10, bf16[128,256]{1,0:T(8,128)(2,1)} %fresh_hbm.1, f32[1,4096]{1,0:T(1,128)} %gain_hbm.1, bf16[8,2,256,256]{3,2,1,0:T(8,128)(2,1)} %bitcast.8, bf16[64,4096]{1,0:T(8,128)(2,1)} %bitcast.9, s32[1,65]{1,0:T(1,128)} %bitcast.11), custom_call_target="tpu_custom_call" | custom-call | tf_op jit(solution)/shard_map/pallas_call | solution.py:325
  61.2 0.6 %copy.8 = bf16[1,128,256]{2,1,0:T(8,128)(2,1)} copy(bf16[1,128,256]{2,1,0:T(8,128)(2,1)S(1)} %bitcast.7) | data formatting | bytes 131072

commit v5 on v4

--- a/solution.py
+++ b/solution.py
@@ -15,6 +15,7 @@
 EPS = 1e-05
 NEG = -1e30
 PIECES = 4
+LINE = 8
 F32 = jnp.float32
 BF16 = jnp.bfloat16
 NT = (((1,), (1,)), ((), ()))
@@ -26,10 +27,11 @@
 
 def body(
     x_hbm, fresh_hbm, gain_hbm, wq_hbm, wkv_hbm, len_hbm, out_ref,
-    xg, xn, wq, wkv_raw, wkv, gain, lens, lens_pad, fresh, first, kvst, kvbuf,
+    xg, xn, wq, wkv_raw, wkv, wkv_quad, gain, lens, lens_pad, fresh, first, kvst, kvbuf,
     acc, sq, part_out, part_in, query_out, query_in, bias1, bias2,
     load_sem, own_sem, swap_send, swap_recv, ring_recv, ring_send, hop_send,
     part_send, part_recv, query_send, query_recv, kv_recv, kv_send, kv_own,
+    quad_send, quad_recv,
 ):
     sections = lax.axis_size("section")
     heads = lax.axis_size("head")
@@ -180,7 +182,8 @@
         sq[...] += low * low + high * high
         scaled = (wide * gain[:, lanes(k, core)]).astype(BF16)
         xn[:, pl.ds(pl.multiple_of(k * width, width), width)] = scaled
-        acc[...] += lax.dot_general(wkv[k], scaled, NT, preferred_element_type=F32)
+        w = wkv[k] if turn == 0 else wkv_quad[k].reshape(2 * columns, width)
+        acc[...] += lax.dot_general(w, scaled, NT, preferred_element_type=F32)
 
     def take_both(turn, k):
         take(turn, -k)
@@ -193,6 +196,29 @@
     pick_key = (same_peer & (sel_c % 16 == sel_r % 8)).astype(F32).astype(BF16)
     pick_value = (same_peer & (sel_c % 16 == 8 + sel_r % 8)).astype(F32).astype(BF16)
     diag = iota((tokens, tokens), 0) == iota((tokens, tokens), 1)
+
+    def share_out(act):
+        part = y % half
+        for m in range(KVH):
+            target = 2 * m + y // half
+            for side, at in ((0, core), (1, 1 - core)):
+                slot = ((part // 2 + core) % 2) * 4 + (part % 2) * 2 + at
+                rows_of = pl.ds(side * columns + m * 16, 16)
+                act(target, wkv.at[:, rows_of], wkv_quad.at[:, slot])
+
+    def start_share(target, src, dst):
+        @pl.when(target == y)
+        def _():
+            pltpu.make_async_copy(src, dst, quad_recv).start()
+
+        @pl.when(target != y)
+        def _():
+            send(src, dst, quad_send, quad_recv, (s, target * 2 + core))
+
+    early = s % LINE == 0
+
+    def share():
+        share_out(start_share)
 
     def exchange(turn):
         square = jnp.sum(sq[...], axis=1, keepdims=True)
@@ -205,6 +231,14 @@
         scale = lax.rsqrt(square * (1.0 / (heads * width)) + EPS)
         total = acc[0:columns] + part_in[turn, 0:columns]
         kvst[turn] = (total * scale).astype(BF16).reshape(KVH, 16, tokens)
+        if turn == 1:
+            quad = h // KVH * KVH
+            mine = kvbuf.at[1, pl.ds(h % KVH * KVH, KVH)]
+            for d in (2, 3, 1):
+                send(kvst.at[1], mine, kv_send.at[1], kv_recv.at[1], (s, quad + (h + d) % KVH))
+            keep = pltpu.make_async_copy(kvst.at[1], mine, kv_own.at[1])
+            keep.start()
+            return scale, keep
         far_first = sorted(range(1 - half, half + 1), key=abs, reverse=True)
         others = [chip(far) * 2 + side for far in far_first if far for side in (core, 1 - core)]
         for other in others + [y * 2 + 1 - core]:
@@ -231,9 +265,11 @@
         ]
         return jnp.concatenate(spread, axis=0).astype(BF16)
 
+    kv_count = (heads - 1, heads - KVH)
+
     def await_kv(turn, keep):
         keep.wait()
-        await_recv(kvbuf.at[turn, pl.ds(0, heads - 1)], kv_recv.at[turn])
+        await_recv(kvbuf.at[turn, pl.ds(0, kv_count[turn])], kv_recv.at[turn])
 
     def attend(turn, wide_q, bias):
         both = [kvbuf[t].reshape(heads * 16, tokens) for t in range(turn + 1)]
@@ -262,7 +298,10 @@
         await_ring(turn, 2)
         if turn == 0:
             order_columns()
+            pl.when(early)(share)
             own.wait()
+        else:
+            await_recv(wkv_quad, quad_recv)
         take(turn, 0)
         await_ring(turn, 1)
         take_both(turn, 1)
@@ -289,6 +328,8 @@
     for p in range(PIECES):
         send(first.at[piece(p)], xg.at[1, y, piece(p)], hop_send, ring_recv.at[1, 0, 0, p], following)
 
+    pl.when(jnp.logical_not(early))(share)
+
     clear()
     for p in range(PIECES):
         await_recv(xg.at[1, y, piece(p)], ring_recv.at[1, 0, 0, p])
@@ -301,13 +342,23 @@
     attend(1, wide_q, bias2)
 
     await_send(first, hop_send)
+    keeps = y % 2 == y // half
+
+    @pl.when(keeps)
+    def _():
+        await_send(wkv_quad.at[:, 0:2 * (KVH - 1)], quad_send)
+
+    @pl.when(jnp.logical_not(keeps))
+    def _():
+        await_send(wkv_quad, quad_send)
+
     await_send(wkv_raw.at[1], swap_send.at[0])
     await_send(wq.at[1], swap_send.at[1])
     for turn in range(2):
         await_send(xg.at[turn, pl.ds(0, 2 * half - 1)], ring_send.at[turn])
         await_send(part_out.at[turn], part_send.at[turn])
         await_send(query_out.at[turn], query_send.at[turn])
-        await_send(kvbuf.at[turn, pl.ds(0, heads - 1)], kv_send.at[turn])
+        await_send(kvbuf.at[turn, pl.ds(0, kv_count[turn])], kv_send.at[turn])
 
 
 def solution(mesh):
@@ -333,6 +384,7 @@
                 vmem((2, chips, width, width), BF16),
                 vmem((2, chips, columns, width), BF16),
                 vmem((chips, 2 * columns, width), BF16),
+                vmem((chips, 2 * KVH, 16, width), BF16),
                 vmem((1, features), F32),
                 vmem((1, docs), jnp.int32),
                 vmem((1, 128), F32),
@@ -362,6 +414,8 @@
                 dma((2,)),
                 dma((2,)),
                 dma((2,)),
+                dma,
+                dma,
             ],
             compiler_params=pltpu.CompilerParams(collective_id=0, has_side_effects=True),
         )(

time: 62 us -> 59.5 us (0.960)
  Pallas kernels: 61.2 us -> 58.8 us
    pallas_call x1, Pallas kernels: 61.2 us -> 58.8 us  [shards(): pl.pallas_call(body, out_shape=pltpu.VMEM((tokens, width), BF16), in_spec...]
where the time goes in v5:
time: 59.5 us; the launch traced here: 59.4 us
  Pallas kernels  58.8 us (99%)
  local copies, waits for them, and re-layouts  0.63 us (1%)
    pallas_call x1, Pallas kernels, shards(): pl.pallas_call(body, out_shape=pltpu.VMEM((tokens, width), BF16), in_spec...  58.8 us

profile of v5, /device:TPU:1, one launch (start us, length us, event | category | flops | bytes accessed | tf_op | source)
XLA Modules:
  0.0 59.4 jit_solution(5687777846776562852)
XLA Ops:
  0.0 58.8 %shard_map.64 = bf16[128,256]{1,0:T(8,128)(2,1)S(1)} custom-call(bf16[128,256]{1,0:T(8,128)(2,1)} %bitcast.10, bf16[128,256]{1,0:T(8,128)(2,1)} %fresh_hbm.1, f32[1,4096]{1,0:T(1,128)} %gain_hbm.1, bf16[8,2,256,256]{3,2,1,0:T(8,128)(2,1)} %bitcast.8, bf16[64,4096]{1,0:T(8,128)(2,1)} %bitcast.9, s32[1,65]{1,0:T(1,128)} %bitcast.11), custom_call_target="tpu_custom_call" | custom-call | tf_op jit(solution)/shard_map/pallas_call | solution.py:376
  58.8 0.6 %copy.8 = bf16[1,128,256]{2,1,0:T(8,128)(2,1)} copy(bf16[1,128,256]{2,1,0:T(8,128)(2,1)S(1)} %bitcast.7) | data formatting | bytes 131072

commit v6 on v5

--- a/solution.py
+++ b/solution.py
@@ -95,7 +95,7 @@
 
     for k in range(chips):
         pltpu.make_async_copy(
-            wkv_hbm.at[:, lanes(k, core)], wkv_raw.at[0, k], load_sem.at[4]
+            wkv_hbm.at[:, lanes(k, core)], wkv_raw.at[k, 0], load_sem.at[4]
         ).start()
     pl.semaphore_wait(barrier, len(greeted))
 
@@ -125,7 +125,7 @@
 
     def swap_weights():
         for k in range(chips):
-            send(wkv_hbm.at[:, lanes(k, 1 - core)], wkv_raw.at[1, k], swap_send.at[0],
+            send(wkv_hbm.at[:, lanes(k, 1 - core)], wkv_raw.at[k, 1], swap_send.at[0],
                  swap_recv.at[0], mate)
         send(wq_hbm.at[:, 1 - core], wq.at[1], swap_send.at[1], swap_recv.at[1], mate)
 
@@ -158,17 +158,15 @@
         bias1[...] = jnp.where(causal & (q1 == k1), 0.0, NEG)
         bias2[:, 0:tokens] = jnp.where(q2 == k1, 0.0, NEG)
         bias2[:, tokens:2 * tokens] = jnp.where(causal & (q2 == k2), 0.0, NEG)
+    r, c = iota((columns, columns), 0), iota((columns, columns), 1)
+    perm = (((c % 8) // 2 == r // 16) & (c // 8 == r % 8) & (c % 2 == (r % 16) // 8))
+    perm = perm.astype(F32).astype(BF16)
+
     def order_columns():
-        r, c = iota((columns, columns), 0), iota((columns, columns), 1)
-        perm = (((c % 8) // 2 == r // 16) & (c // 8 == r % 8) & (c % 2 == (r % 16) // 8))
-        perm = perm.astype(F32).astype(BF16)
-        loads[0].wait()
-        pltpu.make_async_copy(wkv_raw.at[0], wkv_raw.at[0], load_sem.at[4]).wait()
-        await_recv(wkv_raw.at[1], swap_recv.at[0])
         for k in range(chips):
             for side in range(2):
                 wkv[k, side * columns:(side + 1) * columns] = jnp.dot(
-                    perm, wkv_raw[side, k], preferred_element_type=F32
+                    perm, wkv_raw[k, side], preferred_element_type=F32
                 ).astype(BF16)
 
     def clear():
@@ -182,7 +180,7 @@
         sq[...] += low * low + high * high
         scaled = (wide * gain[:, lanes(k, core)]).astype(BF16)
         xn[:, pl.ds(pl.multiple_of(k * width, width), width)] = scaled
-        w = wkv[k] if turn == 0 else wkv_quad[k].reshape(2 * columns, width)
+        w = (wkv_quad if turn else wkv_raw)[k].reshape(2 * columns, width)
         acc[...] += lax.dot_general(w, scaled, NT, preferred_element_type=F32)
 
     def take_both(turn, k):
@@ -218,6 +216,7 @@
     early = s % LINE == 0
 
     def share():
+        order_columns()
         share_out(start_share)
 
     def exchange(turn):
@@ -230,7 +229,10 @@
         square = square + part_in[turn, columns:columns + 1]
         scale = lax.rsqrt(square * (1.0 / (heads * width)) + EPS)
         total = acc[0:columns] + part_in[turn, 0:columns]
-        kvst[turn] = (total * scale).astype(BF16).reshape(KVH, 16, tokens)
+        total = (total * scale).astype(BF16)
+        if turn == 0:
+            total = jnp.dot(perm, total, preferred_element_type=F32).astype(BF16)
+        kvst[turn] = total.reshape(KVH, 16, tokens)
         if turn == 1:
             quad = h // KVH * KVH
             mine = kvbuf.at[1, pl.ds(h % KVH * KVH, KVH)]
@@ -271,18 +273,18 @@
         keep.wait()
         await_recv(kvbuf.at[turn, pl.ds(0, kv_count[turn])], kv_recv.at[turn])
 
-    def attend(turn, wide_q, bias):
-        both = [kvbuf[t].reshape(heads * 16, tokens) for t in range(turn + 1)]
-        scores = [
-            jnp.dot(wide_q, kv, preferred_element_type=F32) * (1.0 / math.sqrt(HD)) for kv in both
-        ]
-        scores = jnp.concatenate(scores, axis=1) + jnp.concatenate([bias[...]] * here, axis=0)
+    def against(turn, wide_q):
+        kv = kvbuf[turn].reshape(heads * 16, tokens)
+        scores = jnp.dot(wide_q, kv, preferred_element_type=F32) * (1.0 / math.sqrt(HD))
+        return scores, jnp.dot(pick_value, kv, preferred_element_type=F32).astype(BF16)
+
+    def attend(turn, wide_q, bias, resident=()):
+        both = [*resident, against(turn, wide_q)]
+        values = jnp.concatenate([v for _, v in both], axis=1)
+        scores = jnp.concatenate([sc for sc, _ in both], axis=1)
+        scores = scores + jnp.concatenate([bias[...]] * here, axis=0)
         expon = jnp.exp(scores - jnp.max(scores, axis=1, keepdims=True))
         weights = (expon / jnp.sum(expon, axis=1, keepdims=True)).astype(BF16)
-        values = [
-            jnp.dot(pick_value, kv, preferred_element_type=F32).astype(BF16) for kv in both
-        ]
-        values = jnp.concatenate(values, axis=1)
         mixed = lax.dot_general(weights, values, NT, preferred_element_type=F32).astype(BF16)
         mixed = mixed.astype(F32)
         for i in range(here):
@@ -295,14 +297,17 @@
                 out_ref[:, cols] = total.astype(BF16)
 
     def rest_of_gather(turn):
+        if turn == 1:
+            await_recv(wkv_quad, quad_recv)
+            take(1, 0)
         await_ring(turn, 2)
         if turn == 0:
-            order_columns()
+            loads[0].wait()
+            pltpu.make_async_copy(wkv_raw.at[:, 0], wkv_raw.at[:, 0], load_sem.at[4]).wait()
+            await_recv(wkv_raw.at[:, 1], swap_recv.at[0])
             pl.when(early)(share)
             own.wait()
-        else:
-            await_recv(wkv_quad, quad_recv)
-        take(turn, 0)
+            take(0, 0)
         await_ring(turn, 1)
         take_both(turn, 1)
         take_both(turn, 2)
@@ -338,8 +343,9 @@
     rest_of_gather(1)
     scale, keep = exchange(1)
     wide_q = queries(1, scale)
+    resident = against(0, wide_q)
     await_kv(1, keep)
-    attend(1, wide_q, bias2)
+    attend(1, wide_q, bias2, [resident])
 
     await_send(first, hop_send)
     keeps = y % 2 == y // half
@@ -352,7 +358,7 @@
     def _():
         await_send(wkv_quad, quad_send)
 
-    await_send(wkv_raw.at[1], swap_send.at[0])
+    await_send(wkv_raw.at[:, 1], swap_send.at[0])
     await_send(wq.at[1], swap_send.at[1])
     for turn in range(2):
         await_send(xg.at[turn, pl.ds(0, 2 * half - 1)], ring_send.at[turn])
@@ -382,7 +388,7 @@
                 vmem((2, chips, tokens, width), BF16),
                 vmem((tokens, features // 2), BF16),
                 vmem((2, chips, width, width), BF16),
-                vmem((2, chips, columns, width), BF16),
+                vmem((chips, 2, columns, width), BF16),
                 vmem((chips, 2 * columns, width), BF16),
                 vmem((chips, 2 * KVH, 16, width), BF16),
                 vmem((1, features), F32),

time: 59.5 us -> 59.5 us (level)
  no operation moved by 1% of the time
where the time goes in v6:
time: 59.5 us; the launch traced here: 59.3 us
  Pallas kernels  58.7 us (99%)
  local copies, waits for them, and re-layouts  0.63 us (1%)
    pallas_call x1, Pallas kernels, shards(): pl.pallas_call(body, out_shape=pltpu.VMEM((tokens, width), BF16), in_spec...  58.7 us

profile of v6, /device:TPU:1, one launch (start us, length us, event | category | flops | bytes accessed | tf_op | source)
XLA Modules:
  0.0 59.3 jit_solution(2570860818884176129)
XLA Ops:
  0.0 58.7 %shard_map.64 = bf16[128,256]{1,0:T(8,128)(2,1)S(1)} custom-call(bf16[128,256]{1,0:T(8,128)(2,1)} %bitcast.10, bf16[128,256]{1,0:T(8,128)(2,1)} %fresh_hbm.1, f32[1,4096]{1,0:T(1,128)} %gain_hbm.1, bf16[8,2,256,256]{3,2,1,0:T(8,128)(2,1)} %bitcast.8, bf16[64,4096]{1,0:T(8,128)(2,1)} %bitcast.9, s32[1,65]{1,0:T(1,128)} %bitcast.11), custom_call_target="tpu_custom_call" | custom-call | tf_op jit(solution)/shard_map/pallas_call | solution.py:382
  58.7 0.6 %copy.8 = bf16[1,128,256]{2,1,0:T(8,128)(2,1)} copy(bf16[1,128,256]{2,1,0:T(8,128)(2,1)S(1)} %bitcast.7) | data formatting | bytes 131072
